TPU v7x, 32 devices: a whole 2x2x4 slice. The times are simulated.
32 devices in a mesh: section: 2 (over y), expert: 8 (over z, x), dp: 2 (over core).
Axes of the slice: x: 2, y: 2, z: 4, core: 2. Of those that a mesh axis runs over, the one named last changes fastest.
Arguments:
- tokens_in: bfloat16 [8, 256, 2048], P(None, ('expert', 'dp')), may hold values from -6 to 6
- cotangent: bfloat16 [8, 256, 2048], P(None, ('expert', 'dp')), may hold values from -4 to 4
- routes: int32 [2, 8, 256, 8], P('section', None, ('expert', 'dp')), may hold values from 0 to 15, all different within a row; in each aligned block of 16 rows (0 to 15, 16 to 31, ..., all dimensions but the last counted through in order) at most 10 rows name the same one
- router_weights: float32 [2, 8, 256, 8], P('section', None, ('expert', 'dp')), may hold values from 0.1 to 0.6
- norm_gain: float32 [2, 2048], P('section'), may hold values from 0.25 to 1.75
- w_gate: bfloat16 [2, 16, 2048, 512], P('section', 'expert'), may hold values from -0.125 to 0.125
- w_up: bfloat16 [2, 16, 2048, 512], P('section', 'expert'), may hold values from -0.125 to 0.125
- w_down: bfloat16 [2, 16, 512, 2048], P('section', 'expert'), may hold values from -0.25 to 0.25
Outputs:
- layer_out: bfloat16 [2, 8, 256, 2048], P('section', None, ('expert', 'dp'))
- input_grad: bfloat16 [2, 8, 256, 2048], P('section', None, ('expert', 'dp'))
- grad_gate: bfloat16 [2, 16, 2048, 512], P('section', 'expert', 'dp')
- grad_up: bfloat16 [2, 16, 2048, 512], P('section', 'expert', 'dp')
- grad_down: bfloat16 [2, 16, 512, 2048], P('section', 'expert', 'dp')
Inputs may be any that keep to these rules, and one draw needn't show every extreme that they name: `routes`: each row names 8 different experts. In each aligned block of 16 rows (the tokens of one device for one layer and one micro-batch) no expert is named by more than 10 rows, and in some blocks one is named by exactly 10.
All inputs are finite; a program needn't handle non-finite values.
Results may differ from a plain program's by a relative error of at most 0.022.
Values may be sent and summed in bfloat16 or wider, within the bound.
A program may use at most 128 MiB of HBM per device.

v0:
```python
import jax
import jax.numpy as jnp
from jax import lax
from jax.sharding import PartitionSpec as P

epsilon = 1e-06


def from_behind(block, axis, distance):
    devices = range(lax.axis_size(axis))
    route = [(i - distance, i) for i in devices if i - distance in devices]
    return lax.ppermute(block, axis, route)


def normalize(hidden, gain_row):
    widened = hidden.astype(jnp.float32)
    inv_rms = lax.rsqrt(jnp.mean(widened * widened, axis=-1, keepdims=True) + epsilon)
    return ((widened * inv_rms * gain_row).astype(jnp.bfloat16), widened, inv_rms)


def routing_tables(route_ids, route_weights, capacity, experts):
    micro_count, token_rows, top_count = route_ids.shape
    assigned = token_rows * top_count
    flat_ids = route_ids.reshape(micro_count, assigned)
    labels = jnp.arange(experts, dtype=jnp.int32)
    onehot = (flat_ids[:, :, None] == labels[None, None, :]).astype(jnp.int32)
    earlier = jnp.cumsum(onehot, axis=1) - onehot
    position = jnp.sum(earlier * onehot, axis=2)
    target = flat_ids * capacity + position
    places = jnp.arange(experts * capacity, dtype=jnp.int32)
    matched = (target[:, None, :] == places[None, :, None]).reshape(
        micro_count, experts * capacity, token_rows, top_count
    )
    selector = jnp.any(matched, axis=3).astype(jnp.bfloat16)
    weighted = jnp.sum(jnp.where(matched, route_weights[:, None, :, :], 0.0), axis=3)
    return (selector, weighted)


def expert_forward(rows_in, gate_w, up_w, down_w):
    gate_pre = jnp.einsum("erx,exf->erf", rows_in, gate_w, preferred_element_type=jnp.float32)
    up_pre = jnp.einsum("erx,exf->erf", rows_in, up_w, preferred_element_type=jnp.float32)
    act_value = (jax.nn.silu(gate_pre) * up_pre).astype(jnp.bfloat16)
    produced = jnp.einsum(
        "erf,efx->erx", act_value, down_w, preferred_element_type=jnp.float32
    ).astype(jnp.bfloat16)
    return (produced, gate_pre, up_pre)


def expert_backward(out_grad, gate_pre, up_pre, gate_w, up_w, down_w):
    act_grad = jnp.einsum("erx,efx->erf", out_grad, down_w, preferred_element_type=jnp.float32)
    sigmoid_g = jax.nn.sigmoid(gate_pre)
    up_grad = (act_grad * gate_pre * sigmoid_g).astype(jnp.bfloat16)
    gate_grad = (act_grad * up_pre * sigmoid_g * (1.0 + gate_pre * (1.0 - sigmoid_g))).astype(
        jnp.bfloat16
    )
    row_grad = jnp.einsum("erf,exf->erx", gate_grad, gate_w, preferred_element_type=jnp.float32)
    row_grad = row_grad + jnp.einsum(
        "erf,exf->erx", up_grad, up_w, preferred_element_type=jnp.float32
    )
    return (row_grad.astype(jnp.bfloat16), gate_grad, up_grad)


def keep_slice(stored, new_value, at_index, is_valid):
    previous = lax.dynamic_index_in_dim(stored, at_index, 0, keepdims=False)
    return lax.dynamic_update_index_in_dim(
        stored, jnp.where(is_valid, new_value, previous), at_index, 0
    )


def round_part(partial_value):
    return lax.optimization_barrier(partial_value.astype(jnp.bfloat16)).astype(jnp.float32)


def send_out(buffer):
    return lax.all_to_all(buffer, "expert", split_axis=0, concat_axis=1, tiled=True)


def send_back(buffer):
    return lax.all_to_all(buffer, "expert", split_axis=1, concat_axis=0, tiled=True)


def on_device(tokens_in, cotangent, routes, router_weights, norm_gain, w_gate, w_up, w_down):
    micro_count, token_rows, model_width = tokens_in.shape
    top_count = routes.shape[3]
    hidden_units = w_gate.shape[3]
    section_count = lax.axis_size("section")
    expert_count = lax.axis_size("expert")
    held_count = w_gate.shape[1]
    experts = held_count * expert_count
    capacity = min(token_rows, 5 * token_rows * top_count // (4 * experts))
    slot_count = experts * capacity
    section_id = lax.axis_index("section")
    selector, weighted = routing_tables(routes[0], router_weights[0], capacity, experts)
    slot_weight = jnp.sum(weighted, axis=2)
    gain_row = norm_gain[0]
    gate_local = w_gate[0]
    up_local = w_up[0]
    down_local = w_down[0]
    expert_rows = expert_count * capacity
    tick_count = section_count + micro_count - 1

    def forward_tick(tick_id, loop_state):
        incoming, inputs_kept, rows_kept, gate_kept, up_kept, outputs_kept = loop_state
        micro_id = tick_id - section_id
        is_valid = jnp.logical_and(micro_id >= 0, micro_id < micro_count)
        clipped = jnp.clip(micro_id, 0, micro_count - 1)
        fresh_in = lax.dynamic_index_in_dim(tokens_in, clipped, 0, keepdims=False)
        hidden = jnp.where(section_id == 0, fresh_in, incoming)
        normed, widened, inv_rms = normalize(hidden, gain_row)
        chooser = lax.dynamic_index_in_dim(selector, clipped, 0, keepdims=False)
        spread = jnp.dot(chooser, normed, preferred_element_type=jnp.float32).astype(jnp.bfloat16)
        arrived = send_out(spread.reshape(experts, capacity, model_width))

        def forward_compute(rows_in):
            return expert_forward(rows_in, gate_local, up_local, down_local)

        def forward_skipped(rows_in):
            return (
                jnp.zeros((held_count, expert_rows, model_width), jnp.bfloat16),
                jnp.zeros((held_count, expert_rows, hidden_units), jnp.float32),
                jnp.zeros((held_count, expert_rows, hidden_units), jnp.float32),
            )

        produced, gate_value, up_value = lax.cond(
            is_valid, forward_compute, forward_skipped, arrived
        )
        returned = send_back(produced).reshape(slot_count, model_width)
        mix_table = lax.dynamic_index_in_dim(weighted, clipped, 0, keepdims=False)
        mixed_sum = widened + jnp.dot(
            mix_table.T,
            returned.astype(jnp.float32),
            precision=lax.Precision.HIGHEST,
            preferred_element_type=jnp.float32,
        )
        output = mixed_sum.astype(jnp.bfloat16)
        inputs_kept = keep_slice(inputs_kept, hidden, clipped, is_valid)
        rows_kept = keep_slice(rows_kept, arrived, clipped, is_valid)
        gate_kept = keep_slice(gate_kept, gate_value, clipped, is_valid)
        up_kept = keep_slice(up_kept, up_value, clipped, is_valid)
        outputs_kept = keep_slice(outputs_kept, output, clipped, is_valid)
        outgoing = from_behind(output, "section", 1)
        return (outgoing, inputs_kept, rows_kept, gate_kept, up_kept, outputs_kept)

    start_state = (
        jnp.zeros((token_rows, model_width), jnp.bfloat16),
        jnp.zeros((micro_count, token_rows, model_width), jnp.bfloat16),
        jnp.zeros((micro_count, held_count, expert_rows, model_width), jnp.bfloat16),
        jnp.zeros((micro_count, held_count, expert_rows, hidden_units), jnp.float32),
        jnp.zeros((micro_count, held_count, expert_rows, hidden_units), jnp.float32),
        jnp.zeros((micro_count, token_rows, model_width), jnp.bfloat16),
    )
    forward_state = lax.fori_loop(0, tick_count, forward_tick, start_state)
    inputs_kept = forward_state[1]
    rows_kept = forward_state[2]
    gate_kept = forward_state[3]
    up_kept = forward_state[4]
    outputs_kept = forward_state[5]

    def backward_tick(tick_id, loop_state):
        incoming, out_kept, gate_grads_kept, up_grads_kept, grads_kept = loop_state
        micro_id = tick_id - (section_count - 1 - section_id)
        is_valid = jnp.logical_and(micro_id >= 0, micro_id < micro_count)
        clipped = jnp.clip(micro_id, 0, micro_count - 1)
        fresh_in = lax.dynamic_index_in_dim(cotangent, clipped, 0, keepdims=False)
        grad_out = jnp.where(section_id == section_count - 1, fresh_in, incoming)
        chooser = lax.dynamic_index_in_dim(selector, clipped, 0, keepdims=False)
        gathered = jnp.dot(chooser, grad_out, preferred_element_type=jnp.float32)
        weight_col = lax.dynamic_index_in_dim(slot_weight, clipped, 0, keepdims=False)
        out_grad = (weight_col[:, None] * gathered).astype(jnp.bfloat16)
        arrived = send_out(out_grad.reshape(experts, capacity, model_width))
        gate_value = lax.dynamic_index_in_dim(gate_kept, clipped, 0, keepdims=False)
        up_value = lax.dynamic_index_in_dim(up_kept, clipped, 0, keepdims=False)

        def backward_compute(operands):
            return expert_backward(
                operands[0], operands[1], operands[2], gate_local, up_local, down_local
            )

        def backward_skipped(operands):
            return (
                jnp.zeros((held_count, expert_rows, model_width), jnp.bfloat16),
                jnp.zeros((held_count, expert_rows, hidden_units), jnp.bfloat16),
                jnp.zeros((held_count, expert_rows, hidden_units), jnp.bfloat16),
            )

        row_grad, gate_grad, up_grad = lax.cond(
            is_valid, backward_compute, backward_skipped, (arrived, gate_value, up_value)
        )
        backed = send_back(row_grad).reshape(slot_count, model_width)
        dnormed = jnp.dot(chooser.T, backed, preferred_element_type=jnp.float32)
        hidden = lax.dynamic_index_in_dim(inputs_kept, clipped, 0, keepdims=False)
        widened = hidden.astype(jnp.float32)
        inv_rms = lax.rsqrt(jnp.mean(widened * widened, axis=-1, keepdims=True) + epsilon)
        unit_rows = widened * inv_rms
        scaled = dnormed * gain_row
        dhidden = grad_out.astype(jnp.float32) + inv_rms * (
            scaled - unit_rows * jnp.mean(scaled * unit_rows, axis=-1, keepdims=True)
        )
        result = dhidden.astype(jnp.bfloat16)
        out_kept = keep_slice(out_kept, arrived, clipped, is_valid)
        gate_grads_kept = keep_slice(gate_grads_kept, gate_grad, clipped, is_valid)
        up_grads_kept = keep_slice(up_grads_kept, up_grad, clipped, is_valid)
        grads_kept = keep_slice(grads_kept, result, clipped, is_valid)
        outgoing = from_behind(result, "section", -1)
        return (outgoing, out_kept, gate_grads_kept, up_grads_kept, grads_kept)

    back_start = (
        jnp.zeros((token_rows, model_width), jnp.bfloat16),
        jnp.zeros((micro_count, held_count, expert_rows, model_width), jnp.bfloat16),
        jnp.zeros((micro_count, held_count, expert_rows, hidden_units), jnp.bfloat16),
        jnp.zeros((micro_count, held_count, expert_rows, hidden_units), jnp.bfloat16),
        jnp.zeros((micro_count, token_rows, model_width), jnp.bfloat16),
    )
    back_state = lax.fori_loop(0, tick_count, backward_tick, back_start)
    out_kept = back_state[1]
    gate_grads_kept = back_state[2]
    up_grads_kept = back_state[3]
    grads_kept = back_state[4]
    act_all = (jax.nn.silu(gate_kept) * up_kept).astype(jnp.bfloat16)
    part_gate = jnp.einsum(
        "merx,merf->exf", rows_kept, gate_grads_kept, preferred_element_type=jnp.float32
    )
    part_up = jnp.einsum(
        "merx,merf->exf", rows_kept, up_grads_kept, preferred_element_type=jnp.float32
    )
    part_down = jnp.einsum("merf,merx->efx", act_all, out_kept, preferred_element_type=jnp.float32)
    summed = (
        lax.psum_scatter(
            round_part(part_gate).astype(jnp.bfloat16), "dp", scatter_dimension=1, tiled=True
        ).astype(jnp.float32),
        lax.psum_scatter(
            round_part(part_up).astype(jnp.bfloat16), "dp", scatter_dimension=1, tiled=True
        ).astype(jnp.float32),
        lax.psum_scatter(
            round_part(part_down).astype(jnp.bfloat16), "dp", scatter_dimension=1, tiled=True
        ).astype(jnp.float32),
    )
    grad_gate = summed[0].astype(jnp.bfloat16)
    grad_up = summed[1].astype(jnp.bfloat16)
    grad_down = summed[2].astype(jnp.bfloat16)
    return (outputs_kept[None], grads_kept[None], grad_gate[None], grad_up[None], grad_down[None])


def solution(mesh):
    placed = (
        P(None, ("expert", "dp"), None),
        P(None, ("expert", "dp"), None),
        P("section", None, ("expert", "dp"), None),
        P("section", None, ("expert", "dp"), None),
        P("section", None),
        P("section", "expert", None, None),
        P("section", "expert", None, None),
        P("section", "expert", None, None),
    )
    return jax.shard_map(
        on_device,
        mesh=mesh,
        in_specs=placed,
        out_specs=(
            P("section", None, ("expert", "dp"), None),
            P("section", None, ("expert", "dp"), None),
            P("section", "expert", "dp", None),
            P("section", "expert", "dp", None),
            P("section", "expert", "dp", None),
        ),
        check_vma=False,
    )
```

profile of v0, /device:TPU:0, one launch (start us, length us, event | category | flops | bytes accessed | tf_op | source)
XLA Modules:
  0.0 1394.0 jit_solution(1228539044011185446)
XLA Ops:
  21.6 651.4 %while.47 = (s32[]{:T(128)}, bf16[16,2048]{1,0:T(8,128)(2,1)S(1)}, bf16[8,16,2048]{2,1,0:T(8,128)(2,1)}, bf16[8,2,80,2048]{3,2,0,1:T(8,128)(2,1)}, f32[8,2,80,51...) while((s32[]{:T(128)}, bf16[16,2048]{1,0:T(8,128)(2,1)S(1)}, ...), condition=%wide.region_8.9_spmd, body=%wide.region_4.0_spmd.sunk | while | flops 1082097664 | bytes 73764016 | solution.py:152
  34.9 23.8 %all-to-all-done = bf16[16,10,2048]{2,1,0:T(8,128)(2,1)S(1)} async-done(((bf16[16,10,2048]{2,1,0:T(8,128)(2,1)}), bf16[16,10,2048]{2,1,0:T(8,128)(2,1)S(1)}, u32[]{:S(2)}, u32[]{:S(2)}) %all-to-all-start) | async-done | bytes 655392 | tf_op jit(solution)/shard_map/while/body/eval_jaxpr/all_to_all | solution.py:75
  77.8 12.8 all-to-all-done.1
  105.2 24.0 %all-to-all-done = bf16[16,10,2048]{2,1,0:T(8,128)(2,1)S(1)} async-done(((bf16[16,10,2048]{2,1,0:T(8,128)(2,1)}), bf16[16,10,2048]{2,1,0:T(8,128)(2,1)S(1)}, u32[]{:S(2)}, u32[]{:S(2)}) %all-to-all-start) | async-done | bytes 655392 | tf_op jit(solution)/shard_map/while/body/eval_jaxpr/all_to_all | solution.py:75
  148.3 12.9 all-to-all-done.1
  177.9 23.7 %all-to-all-done = bf16[16,10,2048]{2,1,0:T(8,128)(2,1)S(1)} async-done(((bf16[16,10,2048]{2,1,0:T(8,128)(2,1)}), bf16[16,10,2048]{2,1,0:T(8,128)(2,1)S(1)}, u32[]{:S(2)}, u32[]{:S(2)}) %all-to-all-start) | async-done | bytes 655392 | tf_op jit(solution)/shard_map/while/body/eval_jaxpr/all_to_all | solution.py:75
  220.7 12.9 all-to-all-done.1
  250.1 23.7 %all-to-all-done = bf16[16,10,2048]{2,1,0:T(8,128)(2,1)S(1)} async-done(((bf16[16,10,2048]{2,1,0:T(8,128)(2,1)}), bf16[16,10,2048]{2,1,0:T(8,128)(2,1)S(1)}, u32[]{:S(2)}, u32[]{:S(2)}) %all-to-all-start) | async-done | bytes 655392 | tf_op jit(solution)/shard_map/while/body/eval_jaxpr/all_to_all | solution.py:75
  292.9 12.9 all-to-all-done.1
  322.2 23.7 %all-to-all-done = bf16[16,10,2048]{2,1,0:T(8,128)(2,1)S(1)} async-done(((bf16[16,10,2048]{2,1,0:T(8,128)(2,1)}), bf16[16,10,2048]{2,1,0:T(8,128)(2,1)S(1)}, u32[]{:S(2)}, u32[]{:S(2)}) %all-to-all-start) | async-done | bytes 655392 | tf_op jit(solution)/shard_map/while/body/eval_jaxpr/all_to_all | solution.py:75
  365.0 12.9 all-to-all-done.1
  394.3 23.7 %all-to-all-done = bf16[16,10,2048]{2,1,0:T(8,128)(2,1)S(1)} async-done(((bf16[16,10,2048]{2,1,0:T(8,128)(2,1)}), bf16[16,10,2048]{2,1,0:T(8,128)(2,1)S(1)}, u32[]{:S(2)}, u32[]{:S(2)}) %all-to-all-start) | async-done | bytes 655392 | tf_op jit(solution)/shard_map/while/body/eval_jaxpr/all_to_all | solution.py:75
  437.1 12.8 all-to-all-done.1
  466.5 23.7 %all-to-all-done = bf16[16,10,2048]{2,1,0:T(8,128)(2,1)S(1)} async-done(((bf16[16,10,2048]{2,1,0:T(8,128)(2,1)}), bf16[16,10,2048]{2,1,0:T(8,128)(2,1)S(1)}, u32[]{:S(2)}, u32[]{:S(2)}) %all-to-all-start) | async-done | bytes 655392 | tf_op jit(solution)/shard_map/while/body/eval_jaxpr/all_to_all | solution.py:75
  509.3 12.9 all-to-all-done.1
  538.6 23.7 %all-to-all-done = bf16[16,10,2048]{2,1,0:T(8,128)(2,1)S(1)} async-done(((bf16[16,10,2048]{2,1,0:T(8,128)(2,1)}), bf16[16,10,2048]{2,1,0:T(8,128)(2,1)S(1)}, u32[]{:S(2)}, u32[]{:S(2)}) %all-to-all-start) | async-done | bytes 655392 | tf_op jit(solution)/shard_map/while/body/eval_jaxpr/all_to_all | solution.py:75
  581.4 12.9 all-to-all-done.1
  610.8 23.7 %all-to-all-done = bf16[16,10,2048]{2,1,0:T(8,128)(2,1)S(1)} async-done(((bf16[16,10,2048]{2,1,0:T(8,128)(2,1)}), bf16[16,10,2048]{2,1,0:T(8,128)(2,1)S(1)}, u32[]{:S(2)}, u32[]{:S(2)}) %all-to-all-start) | async-done | bytes 655392 | tf_op jit(solution)/shard_map/while/body/eval_jaxpr/all_to_all | solution.py:75
  646.5 12.9 all-to-all-done.1
  660.9 10.3 collective-permute-start
  678.5 657.6 %while.48 = (s32[]{:T(128)}, bf16[16,2048]{1,0:T(8,128)(2,1)S(1)}, bf16[8,2,80,2048]{3,2,1,0:T(8,128)(2,1)}, bf16[8,2,80,512]{3,2,0,1:T(8,128)(2,1)}, bf16[8,2,8...) while((s32[]{:T(128)}, bf16[16,2048]{1,0:T(8,128)(2,1)S(1)}, ...), condition=%wide.region_15.16_spmd, body=%wide.region_10.15_spmd.sunk | while | flops 1031094272 | bytes 74154120 | solution.py:214
  686.7 23.2 %all-to-all-done.2 = bf16[16,10,2048]{2,1,0:T(8,128)(2,1)S(1)} async-done(((bf16[16,10,2048]{2,1,0:T(8,128)(2,1)}), bf16[16,10,2048]{2,1,0:T(8,128)(2,1)S(1)}, u32[]{:S(2)}, u32[]{:S(2)}) %all-to-all-start.2) | async-done | bytes 655392 | tf_op jit(solution)/shard_map/while/body/eval_jaxpr/all_to_all | solution.py:75
  721.5 12.8 all-to-all-done.3
  739.1 12.1 collective-permute-done.1
  759.4 23.4 %all-to-all-done.2 = bf16[16,10,2048]{2,1,0:T(8,128)(2,1)S(1)} async-done(((bf16[16,10,2048]{2,1,0:T(8,128)(2,1)}), bf16[16,10,2048]{2,1,0:T(8,128)(2,1)S(1)}, u32[]{:S(2)}, u32[]{:S(2)}) %all-to-all-start.2) | async-done | bytes 655392 | tf_op jit(solution)/shard_map/while/body/eval_jaxpr/all_to_all | solution.py:75
  803.2 12.8 all-to-all-done.3
  833.0 22.9 %all-to-all-done.2 = bf16[16,10,2048]{2,1,0:T(8,128)(2,1)S(1)} async-done(((bf16[16,10,2048]{2,1,0:T(8,128)(2,1)}), bf16[16,10,2048]{2,1,0:T(8,128)(2,1)S(1)}, u32[]{:S(2)}, u32[]{:S(2)}) %all-to-all-start.2) | async-done | bytes 655392 | tf_op jit(solution)/shard_map/while/body/eval_jaxpr/all_to_all | solution.py:75
  856.6 10.1 conditional.5
  876.3 12.8 all-to-all-done.3
  906.1 22.9 %all-to-all-done.2 = bf16[16,10,2048]{2,1,0:T(8,128)(2,1)S(1)} async-done(((bf16[16,10,2048]{2,1,0:T(8,128)(2,1)}), bf16[16,10,2048]{2,1,0:T(8,128)(2,1)S(1)}, u32[]{:S(2)}, u32[]{:S(2)}) %all-to-all-start.2) | async-done | bytes 655392 | tf_op jit(solution)/shard_map/while/body/eval_jaxpr/all_to_all | solution.py:75
  929.6 10.1 conditional.5
  949.3 12.8 all-to-all-done.3
  979.1 22.9 %all-to-all-done.2 = bf16[16,10,2048]{2,1,0:T(8,128)(2,1)S(1)} async-done(((bf16[16,10,2048]{2,1,0:T(8,128)(2,1)}), bf16[16,10,2048]{2,1,0:T(8,128)(2,1)S(1)}, u32[]{:S(2)}, u32[]{:S(2)}) %all-to-all-start.2) | async-done | bytes 655392 | tf_op jit(solution)/shard_map/while/body/eval_jaxpr/all_to_all | solution.py:75
  1002.7 10.1 conditional.5
  1022.3 12.9 all-to-all-done.3
  1052.1 22.9 %all-to-all-done.2 = bf16[16,10,2048]{2,1,0:T(8,128)(2,1)S(1)} async-done(((bf16[16,10,2048]{2,1,0:T(8,128)(2,1)}), bf16[16,10,2048]{2,1,0:T(8,128)(2,1)S(1)}, u32[]{:S(2)}, u32[]{:S(2)}) %all-to-all-start.2) | async-done | bytes 655392 | tf_op jit(solution)/shard_map/while/body/eval_jaxpr/all_to_all | solution.py:75
  1075.7 10.1 conditional.5
  1095.4 12.8 all-to-all-done.3
  1125.2 22.9 %all-to-all-done.2 = bf16[16,10,2048]{2,1,0:T(8,128)(2,1)S(1)} async-done(((bf16[16,10,2048]{2,1,0:T(8,128)(2,1)}), bf16[16,10,2048]{2,1,0:T(8,128)(2,1)S(1)}, u32[]{:S(2)}, u32[]{:S(2)}) %all-to-all-start.2) | async-done | bytes 655392 | tf_op jit(solution)/shard_map/while/body/eval_jaxpr/all_to_all | solution.py:75
  1148.7 10.1 conditional.5
  1168.5 12.8 all-to-all-done.3
  1198.2 22.9 %all-to-all-done.2 = bf16[16,10,2048]{2,1,0:T(8,128)(2,1)S(1)} async-done(((bf16[16,10,2048]{2,1,0:T(8,128)(2,1)}), bf16[16,10,2048]{2,1,0:T(8,128)(2,1)S(1)}, u32[]{:S(2)}, u32[]{:S(2)}) %all-to-all-start.2) | async-done | bytes 655392 | tf_op jit(solution)/shard_map/while/body/eval_jaxpr/all_to_all | solution.py:75
  1221.8 10.1 conditional.5
  1241.4 12.8 all-to-all-done.3
  1271.3 22.9 %all-to-all-done.2 = bf16[16,10,2048]{2,1,0:T(8,128)(2,1)S(1)} async-done(((bf16[16,10,2048]{2,1,0:T(8,128)(2,1)}), bf16[16,10,2048]{2,1,0:T(8,128)(2,1)S(1)}, u32[]{:S(2)}, u32[]{:S(2)}) %all-to-all-start.2) | async-done | bytes 655392 | tf_op jit(solution)/shard_map/while/body/eval_jaxpr/all_to_all | solution.py:75
  1294.8 10.1 conditional.5
  1314.4 12.9 all-to-all-done.3
  1371.2 16.2 %reduce-scatter.8.cloned.1.call-done = bf16[2,256,2048]{2,1,0:T(8,128)(2,1)} async-done(((bf16[2,512,2048]{2,1,0:T(8,128)(2,1)}), bf16[2,256,2048]{2,1,0:T(8,128)(2,1)}) %reduce-scatter.8.cloned.1.call-update) | async-done | bytes 2097168 | tf_op jit(solution)/shard_map/reduce_scatter | solution.py:234
  (605 shorter events, 770.3 us)
Async XLA Ops:
  7.2 1357.9 %reduce-scatter.6.cloned.1.call-start = ((), (), s32[]{:S(2)}) async-start(), calls=%async_computation.8 | async-start | bytes 6291456 | tf_op jit(solution)/shard_map/reduce_scatter | solution.py:231
  25.7 33.0 %all-to-all-start = ((bf16[16,10,2048]{2,1,0:T(8,128)(2,1)}), bf16[16,10,2048]{2,1,0:T(8,128)(2,1)S(1)}, u32[]{:S(2)}, u32[]{:S(2)}) async-start(bf16[16,10,2048]{2,1,0:T(8,128)(2,1)} %reshape.112), calls=%async_computation | async-start | bytes 2097152 | tf_op jit(solution)/shard_map/while/body/eval_jaxpr/all_to_all | solution.py:75
  69.6 21.1 %all-to-all-start.1 = ((bf16[2,80,2048]{2,0,1:T(2,128)(2,1)}), bf16[2,80,2048]{2,0,1:T(2,128)(2,1)S(1)}, u32[]{:S(2)}, u32[]{:S(2)}) async-start(bf16[2,80,2048]{2,0,1:T(2,128)(2,1)} %copy.142), calls=%async_computation.1 | async-start | bytes 1310720 | tf_op jit(solution)/shard_map/while/body/eval_jaxpr/all_to_all | solution.py:79
  99.6 29.6 %all-to-all-start = ((bf16[16,10,2048]{2,1,0:T(8,128)(2,1)}), bf16[16,10,2048]{2,1,0:T(8,128)(2,1)S(1)}, u32[]{:S(2)}, u32[]{:S(2)}) async-start(bf16[16,10,2048]{2,1,0:T(8,128)(2,1)} %reshape.112), calls=%async_computation | async-start | bytes 2097152 | tf_op jit(solution)/shard_map/while/body/eval_jaxpr/all_to_all | solution.py:75
  140.1 21.1 %all-to-all-start.1 = ((bf16[2,80,2048]{2,0,1:T(2,128)(2,1)}), bf16[2,80,2048]{2,0,1:T(2,128)(2,1)S(1)}, u32[]{:S(2)}, u32[]{:S(2)}) async-start(bf16[2,80,2048]{2,0,1:T(2,128)(2,1)} %copy.142), calls=%async_computation.1 | async-start | bytes 1310720 | tf_op jit(solution)/shard_map/while/body/eval_jaxpr/all_to_all | solution.py:79
  172.3 29.3 %all-to-all-start = ((bf16[16,10,2048]{2,1,0:T(8,128)(2,1)}), bf16[16,10,2048]{2,1,0:T(8,128)(2,1)S(1)}, u32[]{:S(2)}, u32[]{:S(2)}) async-start(bf16[16,10,2048]{2,1,0:T(8,128)(2,1)} %reshape.112), calls=%async_computation | async-start | bytes 2097152 | tf_op jit(solution)/shard_map/while/body/eval_jaxpr/all_to_all | solution.py:75
  212.5 21.0 %all-to-all-start.1 = ((bf16[2,80,2048]{2,0,1:T(2,128)(2,1)}), bf16[2,80,2048]{2,0,1:T(2,128)(2,1)S(1)}, u32[]{:S(2)}, u32[]{:S(2)}) async-start(bf16[2,80,2048]{2,0,1:T(2,128)(2,1)} %copy.142), calls=%async_computation.1 | async-start | bytes 1310720 | tf_op jit(solution)/shard_map/while/body/eval_jaxpr/all_to_all | solution.py:79
  244.5 29.3 %all-to-all-start = ((bf16[16,10,2048]{2,1,0:T(8,128)(2,1)}), bf16[16,10,2048]{2,1,0:T(8,128)(2,1)S(1)}, u32[]{:S(2)}, u32[]{:S(2)}) async-start(bf16[16,10,2048]{2,1,0:T(8,128)(2,1)} %reshape.112), calls=%async_computation | async-start | bytes 2097152 | tf_op jit(solution)/shard_map/while/body/eval_jaxpr/all_to_all | solution.py:75
  284.8 21.0 %all-to-all-start.1 = ((bf16[2,80,2048]{2,0,1:T(2,128)(2,1)}), bf16[2,80,2048]{2,0,1:T(2,128)(2,1)S(1)}, u32[]{:S(2)}, u32[]{:S(2)}) async-start(bf16[2,80,2048]{2,0,1:T(2,128)(2,1)} %copy.142), calls=%async_computation.1 | async-start | bytes 1310720 | tf_op jit(solution)/shard_map/while/body/eval_jaxpr/all_to_all | solution.py:79
  316.6 29.3 %all-to-all-start = ((bf16[16,10,2048]{2,1,0:T(8,128)(2,1)}), bf16[16,10,2048]{2,1,0:T(8,128)(2,1)S(1)}, u32[]{:S(2)}, u32[]{:S(2)}) async-start(bf16[16,10,2048]{2,1,0:T(8,128)(2,1)} %reshape.112), calls=%async_computation | async-start | bytes 2097152 | tf_op jit(solution)/shard_map/while/body/eval_jaxpr/all_to_all | solution.py:75
  356.8 21.0 %all-to-all-start.1 = ((bf16[2,80,2048]{2,0,1:T(2,128)(2,1)}), bf16[2,80,2048]{2,0,1:T(2,128)(2,1)S(1)}, u32[]{:S(2)}, u32[]{:S(2)}) async-start(bf16[2,80,2048]{2,0,1:T(2,128)(2,1)} %copy.142), calls=%async_computation.1 | async-start | bytes 1310720 | tf_op jit(solution)/shard_map/while/body/eval_jaxpr/all_to_all | solution.py:79
  388.7 29.3 %all-to-all-start = ((bf16[16,10,2048]{2,1,0:T(8,128)(2,1)}), bf16[16,10,2048]{2,1,0:T(8,128)(2,1)S(1)}, u32[]{:S(2)}, u32[]{:S(2)}) async-start(bf16[16,10,2048]{2,1,0:T(8,128)(2,1)} %reshape.112), calls=%async_computation | async-start | bytes 2097152 | tf_op jit(solution)/shard_map/while/body/eval_jaxpr/all_to_all | solution.py:75
  428.9 21.0 %all-to-all-start.1 = ((bf16[2,80,2048]{2,0,1:T(2,128)(2,1)}), bf16[2,80,2048]{2,0,1:T(2,128)(2,1)S(1)}, u32[]{:S(2)}, u32[]{:S(2)}) async-start(bf16[2,80,2048]{2,0,1:T(2,128)(2,1)} %copy.142), calls=%async_computation.1 | async-start | bytes 1310720 | tf_op jit(solution)/shard_map/while/body/eval_jaxpr/all_to_all | solution.py:79
  460.9 29.3 %all-to-all-start = ((bf16[16,10,2048]{2,1,0:T(8,128)(2,1)}), bf16[16,10,2048]{2,1,0:T(8,128)(2,1)S(1)}, u32[]{:S(2)}, u32[]{:S(2)}) async-start(bf16[16,10,2048]{2,1,0:T(8,128)(2,1)} %reshape.112), calls=%async_computation | async-start | bytes 2097152 | tf_op jit(solution)/shard_map/while/body/eval_jaxpr/all_to_all | solution.py:75
  501.1 21.0 %all-to-all-start.1 = ((bf16[2,80,2048]{2,0,1:T(2,128)(2,1)}), bf16[2,80,2048]{2,0,1:T(2,128)(2,1)S(1)}, u32[]{:S(2)}, u32[]{:S(2)}) async-start(bf16[2,80,2048]{2,0,1:T(2,128)(2,1)} %copy.142), calls=%async_computation.1 | async-start | bytes 1310720 | tf_op jit(solution)/shard_map/while/body/eval_jaxpr/all_to_all | solution.py:79
  533.0 29.3 %all-to-all-start = ((bf16[16,10,2048]{2,1,0:T(8,128)(2,1)}), bf16[16,10,2048]{2,1,0:T(8,128)(2,1)S(1)}, u32[]{:S(2)}, u32[]{:S(2)}) async-start(bf16[16,10,2048]{2,1,0:T(8,128)(2,1)} %reshape.112), calls=%async_computation | async-start | bytes 2097152 | tf_op jit(solution)/shard_map/while/body/eval_jaxpr/all_to_all | solution.py:75
  573.2 21.0 %all-to-all-start.1 = ((bf16[2,80,2048]{2,0,1:T(2,128)(2,1)}), bf16[2,80,2048]{2,0,1:T(2,128)(2,1)S(1)}, u32[]{:S(2)}, u32[]{:S(2)}) async-start(bf16[2,80,2048]{2,0,1:T(2,128)(2,1)} %copy.142), calls=%async_computation.1 | async-start | bytes 1310720 | tf_op jit(solution)/shard_map/while/body/eval_jaxpr/all_to_all | solution.py:79
  605.2 29.3 %all-to-all-start = ((bf16[16,10,2048]{2,1,0:T(8,128)(2,1)}), bf16[16,10,2048]{2,1,0:T(8,128)(2,1)S(1)}, u32[]{:S(2)}, u32[]{:S(2)}) async-start(bf16[16,10,2048]{2,1,0:T(8,128)(2,1)} %reshape.112), calls=%async_computation | async-start | bytes 2097152 | tf_op jit(solution)/shard_map/while/body/eval_jaxpr/all_to_all | solution.py:75
  638.3 21.0 %all-to-all-start.1 = ((bf16[2,80,2048]{2,0,1:T(2,128)(2,1)}), bf16[2,80,2048]{2,0,1:T(2,128)(2,1)S(1)}, u32[]{:S(2)}, u32[]{:S(2)}) async-start(bf16[2,80,2048]{2,0,1:T(2,128)(2,1)} %copy.142), calls=%async_computation.1 | async-start | bytes 1310720 | tf_op jit(solution)/shard_map/while/body/eval_jaxpr/all_to_all | solution.py:79
  660.9 12.2 collective-permute-start
  680.9 29.0 %all-to-all-start.2 = ((bf16[16,10,2048]{2,1,0:T(8,128)(2,1)}), bf16[16,10,2048]{2,1,0:T(8,128)(2,1)S(1)}, u32[]{:S(2)}, u32[]{:S(2)}) async-start(bf16[16,10,2048]{2,1,0:T(8,128)(2,1)} %reshape.114), calls=%async_computation.2 | async-start | bytes 2097152 | tf_op jit(solution)/shard_map/while/body/eval_jaxpr/all_to_all | solution.py:75
  713.5 20.8 %all-to-all-start.3 = ((bf16[2,80,2048]{2,0,1:T(2,128)(2,1)}), bf16[2,80,2048]{2,0,1:T(2,128)(2,1)S(1)}, u32[]{:S(2)}, u32[]{:S(2)}) async-start(bf16[2,80,2048]{2,0,1:T(2,128)(2,1)} %copy.148), calls=%async_computation.3 | async-start | bytes 1310720 | tf_op jit(solution)/shard_map/while/body/eval_jaxpr/all_to_all | solution.py:79
  737.0 14.2 %collective-permute-start.1 = (bf16[16,2048]{1,0:T(8,128)(2,1)S(1)}, bf16[16,2048]{1,0:T(8,128)(2,1)S(1)}, u32[]{:S(2)}, u32[]{:S(2)}) collective-permute-start(bf16[16,2048]{1,0:T(8,128)(2,1)S(1)} %get-tuple-element.1148), channel_id=1, source_target_pairs={{16,0},{17,1},{18,2},{19,3},{20,4},{21,5},{22,6},{23,7},{24,8},{25... | collective-permute-start | bytes 196616 | tf_op jit(solution)/shard_map/while/body/eval_jaxpr/ppermute | solution.py:12
  753.6 29.2 %all-to-all-start.2 = ((bf16[16,10,2048]{2,1,0:T(8,128)(2,1)}), bf16[16,10,2048]{2,1,0:T(8,128)(2,1)S(1)}, u32[]{:S(2)}, u32[]{:S(2)}) async-start(bf16[16,10,2048]{2,1,0:T(8,128)(2,1)} %reshape.114), calls=%async_computation.2 | async-start | bytes 2097152 | tf_op jit(solution)/shard_map/while/body/eval_jaxpr/all_to_all | solution.py:75
  795.1 20.9 %all-to-all-start.3 = ((bf16[2,80,2048]{2,0,1:T(2,128)(2,1)}), bf16[2,80,2048]{2,0,1:T(2,128)(2,1)S(1)}, u32[]{:S(2)}, u32[]{:S(2)}) async-start(bf16[2,80,2048]{2,0,1:T(2,128)(2,1)} %copy.148), calls=%async_computation.3 | async-start | bytes 1310720 | tf_op jit(solution)/shard_map/while/body/eval_jaxpr/all_to_all | solution.py:79
  818.7 6.2 collective-permute-start.1
  827.3 28.7 %all-to-all-start.2 = ((bf16[16,10,2048]{2,1,0:T(8,128)(2,1)}), bf16[16,10,2048]{2,1,0:T(8,128)(2,1)S(1)}, u32[]{:S(2)}, u32[]{:S(2)}) async-start(bf16[16,10,2048]{2,1,0:T(8,128)(2,1)} %reshape.114), calls=%async_computation.2 | async-start | bytes 2097152 | tf_op jit(solution)/shard_map/while/body/eval_jaxpr/all_to_all | solution.py:75
  868.2 20.9 %all-to-all-start.3 = ((bf16[2,80,2048]{2,0,1:T(2,128)(2,1)}), bf16[2,80,2048]{2,0,1:T(2,128)(2,1)S(1)}, u32[]{:S(2)}, u32[]{:S(2)}) async-start(bf16[2,80,2048]{2,0,1:T(2,128)(2,1)} %copy.148), calls=%async_computation.3 | async-start | bytes 1310720 | tf_op jit(solution)/shard_map/while/body/eval_jaxpr/all_to_all | solution.py:79
  891.8 6.2 collective-permute-start.1
  900.3 28.7 %all-to-all-start.2 = ((bf16[16,10,2048]{2,1,0:T(8,128)(2,1)}), bf16[16,10,2048]{2,1,0:T(8,128)(2,1)S(1)}, u32[]{:S(2)}, u32[]{:S(2)}) async-start(bf16[16,10,2048]{2,1,0:T(8,128)(2,1)} %reshape.114), calls=%async_computation.2 | async-start | bytes 2097152 | tf_op jit(solution)/shard_map/while/body/eval_jaxpr/all_to_all | solution.py:75
  941.3 20.9 %all-to-all-start.3 = ((bf16[2,80,2048]{2,0,1:T(2,128)(2,1)}), bf16[2,80,2048]{2,0,1:T(2,128)(2,1)S(1)}, u32[]{:S(2)}, u32[]{:S(2)}) async-start(bf16[2,80,2048]{2,0,1:T(2,128)(2,1)} %copy.148), calls=%async_computation.3 | async-start | bytes 1310720 | tf_op jit(solution)/shard_map/while/body/eval_jaxpr/all_to_all | solution.py:79
  964.8 6.2 collective-permute-start.1
  973.3 28.7 %all-to-all-start.2 = ((bf16[16,10,2048]{2,1,0:T(8,128)(2,1)}), bf16[16,10,2048]{2,1,0:T(8,128)(2,1)S(1)}, u32[]{:S(2)}, u32[]{:S(2)}) async-start(bf16[16,10,2048]{2,1,0:T(8,128)(2,1)} %reshape.114), calls=%async_computation.2 | async-start | bytes 2097152 | tf_op jit(solution)/shard_map/while/body/eval_jaxpr/all_to_all | solution.py:75
  1014.3 20.9 %all-to-all-start.3 = ((bf16[2,80,2048]{2,0,1:T(2,128)(2,1)}), bf16[2,80,2048]{2,0,1:T(2,128)(2,1)S(1)}, u32[]{:S(2)}, u32[]{:S(2)}) async-start(bf16[2,80,2048]{2,0,1:T(2,128)(2,1)} %copy.148), calls=%async_computation.3 | async-start | bytes 1310720 | tf_op jit(solution)/shard_map/while/body/eval_jaxpr/all_to_all | solution.py:79
  1037.8 6.2 collective-permute-start.1
  1046.4 28.7 %all-to-all-start.2 = ((bf16[16,10,2048]{2,1,0:T(8,128)(2,1)}), bf16[16,10,2048]{2,1,0:T(8,128)(2,1)S(1)}, u32[]{:S(2)}, u32[]{:S(2)}) async-start(bf16[16,10,2048]{2,1,0:T(8,128)(2,1)} %reshape.114), calls=%async_computation.2 | async-start | bytes 2097152 | tf_op jit(solution)/shard_map/while/body/eval_jaxpr/all_to_all | solution.py:75
  1087.3 20.9 %all-to-all-start.3 = ((bf16[2,80,2048]{2,0,1:T(2,128)(2,1)}), bf16[2,80,2048]{2,0,1:T(2,128)(2,1)S(1)}, u32[]{:S(2)}, u32[]{:S(2)}) async-start(bf16[2,80,2048]{2,0,1:T(2,128)(2,1)} %copy.148), calls=%async_computation.3 | async-start | bytes 1310720 | tf_op jit(solution)/shard_map/while/body/eval_jaxpr/all_to_all | solution.py:79
  1110.9 6.2 collective-permute-start.1
  1119.4 28.7 %all-to-all-start.2 = ((bf16[16,10,2048]{2,1,0:T(8,128)(2,1)}), bf16[16,10,2048]{2,1,0:T(8,128)(2,1)S(1)}, u32[]{:S(2)}, u32[]{:S(2)}) async-start(bf16[16,10,2048]{2,1,0:T(8,128)(2,1)} %reshape.114), calls=%async_computation.2 | async-start | bytes 2097152 | tf_op jit(solution)/shard_map/while/body/eval_jaxpr/all_to_all | solution.py:75
  1160.4 20.9 %all-to-all-start.3 = ((bf16[2,80,2048]{2,0,1:T(2,128)(2,1)}), bf16[2,80,2048]{2,0,1:T(2,128)(2,1)S(1)}, u32[]{:S(2)}, u32[]{:S(2)}) async-start(bf16[2,80,2048]{2,0,1:T(2,128)(2,1)} %copy.148), calls=%async_computation.3 | async-start | bytes 1310720 | tf_op jit(solution)/shard_map/while/body/eval_jaxpr/all_to_all | solution.py:79
  1183.9 6.2 collective-permute-start.1
  1192.4 28.7 %all-to-all-start.2 = ((bf16[16,10,2048]{2,1,0:T(8,128)(2,1)}), bf16[16,10,2048]{2,1,0:T(8,128)(2,1)S(1)}, u32[]{:S(2)}, u32[]{:S(2)}) async-start(bf16[16,10,2048]{2,1,0:T(8,128)(2,1)} %reshape.114), calls=%async_computation.2 | async-start | bytes 2097152 | tf_op jit(solution)/shard_map/while/body/eval_jaxpr/all_to_all | solution.py:75
  1233.4 20.9 %all-to-all-start.3 = ((bf16[2,80,2048]{2,0,1:T(2,128)(2,1)}), bf16[2,80,2048]{2,0,1:T(2,128)(2,1)S(1)}, u32[]{:S(2)}, u32[]{:S(2)}) async-start(bf16[2,80,2048]{2,0,1:T(2,128)(2,1)} %copy.148), calls=%async_computation.3 | async-start | bytes 1310720 | tf_op jit(solution)/shard_map/while/body/eval_jaxpr/all_to_all | solution.py:79
  1256.9 6.2 collective-permute-start.1
  1265.5 28.7 %all-to-all-start.2 = ((bf16[16,10,2048]{2,1,0:T(8,128)(2,1)}), bf16[16,10,2048]{2,1,0:T(8,128)(2,1)S(1)}, u32[]{:S(2)}, u32[]{:S(2)}) async-start(bf16[16,10,2048]{2,1,0:T(8,128)(2,1)} %reshape.114), calls=%async_computation.2 | async-start | bytes 2097152 | tf_op jit(solution)/shard_map/while/body/eval_jaxpr/all_to_all | solution.py:75
  1306.4 20.9 %all-to-all-start.3 = ((bf16[2,80,2048]{2,0,1:T(2,128)(2,1)}), bf16[2,80,2048]{2,0,1:T(2,128)(2,1)S(1)}, u32[]{:S(2)}, u32[]{:S(2)}) async-start(bf16[2,80,2048]{2,0,1:T(2,128)(2,1)} %copy.148), calls=%async_computation.3 | async-start | bytes 1310720 | tf_op jit(solution)/shard_map/while/body/eval_jaxpr/all_to_all | solution.py:79
  1344.7 26.6 %reduce-scatter.4.cloned.1.call-start = ((), (), s32[]{:S(2)}) async-start(), calls=%async_computation.7 | async-start | bytes 6291456 | tf_op jit(solution)/shard_map/reduce_scatter | solution.py:228
  1354.4 33.0 %reduce-scatter.8.cloned.1.call-start = ((), (), s32[]{:S(2)}) async-start(), calls=%async_computation.9 | async-start | bytes 6291456 | tf_op jit(solution)/shard_map/reduce_scatter | solution.py:234
  (45 other events, 169.2 us)
Sparse Core Ops, SparseCore 0:
  1344.8 10.1 reduce-scatter.5
  1357.9 13.3 reduce-scatter.3
  1374.1 13.3 reduce-scatter.7
where the time goes:
time: 1400 us; the launch traced here: 1390 us
  waiting for transfers between devices  712 us (51%)
  local copies, waits for them, and re-layouts  208 us (15%)
  matrix products  195 us (14%)
  starting transfers between devices  179 us (13%)
  other arithmetic  83.9 us (6%)
    all_to_all x18, waiting for transfers between devices, send_out(): lax.all_to_all(buffer, 'expert', split_axis=0, concat_axis=1, tiled=True)  421 us
    all_to_all x18, waiting for transfers between devices, send_back(): lax.all_to_all(buffer, 'expert', split_axis=1, concat_axis=0, tiled=True)  231 us
    dynamic_slice x81, local copies, waits for them, and re-layouts, keep_slice(): previous = lax.dynamic_index_in_dim(stored, at_index, 0, keepdims=False)  70.5 us
    all_to_all x18, starting transfers between devices, send_out(): lax.all_to_all(buffer, 'expert', split_axis=0, concat_axis=1, tiled=True)  69.2 us
    all_to_all x18, starting transfers between devices, send_back(): lax.all_to_all(buffer, 'expert', split_axis=1, concat_axis=0, tiled=True)  64.1 us
    dynamic_update_slice x36, other arithmetic, keep_slice(): lax.dynamic_update_index_in_dim(stored, jnp.where(is_valid, new_value, pr...  55.1 us
    ppermute x18, starting transfers between devices, from_behind(): return lax.ppermute(block, axis, route)  46.1 us
    dot_general x8, matrix products, expert_backward(): jnp.einsum('erx,efx->erf', out_grad, down_w, preferred_element_type=jnp.f...  38.1 us
  transfers between devices with their start and end apart: 57, of which 48 were waited for; matrix products, arithmetic and copies ran while one was open for 12% of the time, Pallas kernels for 0%

commit v1 on v0

v1 whole, which is shorter than its diff:
```python
import jax
import jax.numpy as jnp
from jax import lax
from jax.sharding import PartitionSpec as P

epsilon = 1e-06
ROW_LIMIT = 1024


def from_behind(block, axis, distance):
    devices = range(lax.axis_size(axis))
    route = [(i - distance, i) for i in devices if i - distance in devices]
    return lax.ppermute(block, axis, route)


def pick(section_id, by_section):
    entries = list(by_section.items())
    chosen = entries[0][1]
    for section, value in entries[1:]:
        if value is not chosen:
            chosen = jnp.where(section_id == section, value, chosen)
    return chosen


def weight_table(route_ids, route_weights, experts, expert_count):
    labels = jnp.arange(experts, dtype=jnp.int32)[:, None, None, None]
    dense = jnp.sum(jnp.where(route_ids[None] == labels, route_weights[None], 0.0), axis=3)
    dense = dense.reshape((expert_count, experts // expert_count) + dense.shape[1:])
    return lax.all_to_all(dense, "expert", split_axis=0, concat_axis=0, tiled=True)


def on_device(tokens_in, cotangent, routes, router_weights, norm_gain, w_gate, w_up, w_down):
    micro_count, token_rows, width = tokens_in.shape
    held, hidden_units = w_gate.shape[1], w_gate.shape[3]
    sections = lax.axis_size("section")
    expert_count = lax.axis_size("expert")
    dp_count = lax.axis_size("dp")
    chunks = 1
    while micro_count % (2 * chunks) == 0 and micro_count * token_rows * expert_count > ROW_LIMIT * chunks:
        chunks *= 2
    per_chunk = micro_count // chunks
    own_rows = per_chunk * token_rows
    ticks = sections + chunks - 1
    inner = held * hidden_units
    section_id = lax.axis_index("section")
    gain_row = norm_gain[0]
    table = weight_table(routes[0], router_weights[0], held * expert_count, expert_count)
    w_in = jnp.concatenate([w_gate[0, e] for e in range(held)] + [w_up[0, e] for e in range(held)], axis=1)
    w_out = w_down[0].reshape(inner, width)

    def chunk_of(array, chunk, axis):
        if chunks == 1:
            return array
        return lax.dynamic_slice_in_dim(array, chunk * per_chunk, per_chunk, axis)

    def spread_weights(chunk):
        rows = chunk_of(table, chunk, 2).transpose(0, 2, 3, 1).reshape(-1, held)
        return jnp.repeat(rows, hidden_units, axis=1)

    def gather(rows):
        return lax.all_gather(rows, "expert", axis=0, tiled=True)

    def scatter(rows):
        return lax.psum_scatter(rows, "expert", scatter_dimension=0, tiled=True)

    def rms(hidden):
        widened = hidden.astype(jnp.float32)
        return widened, lax.rsqrt(jnp.mean(widened * widened, axis=-1, keepdims=True) + epsilon)

    compact = sections > 2

    def keep(store, value, owner):
        if not compact:
            store.append(value)
        elif not store:
            store.extend([value] * chunks)
        else:
            store[:] = [jnp.where(section_id == owner(c), value, old) for c, old in enumerate(store)]
            store[:] = lax.optimization_barrier(store)

    def at(store, chunk, shift):
        return store[chunk] if compact else store[chunk + shift]

    hiddens, rows_in, pre_acts, acts, outputs = [], [], [], [], []
    incoming = None
    for tick in range(ticks):
        chunk = jnp.clip(tick - section_id, 0, chunks - 1)
        hidden = None
        if tick < chunks:
            hidden = chunk_of(tokens_in, chunk, 0).reshape(own_rows, width)
        if tick > 0:
            hidden = incoming if hidden is None else jnp.where(section_id == 0, hidden, incoming)
        widened, inv_rms = rms(hidden)
        gathered = gather((widened * inv_rms * gain_row).astype(jnp.bfloat16))
        pre = jnp.dot(gathered, w_in, preferred_element_type=jnp.float32).astype(jnp.bfloat16)
        gate, up = pre[:, :inner].astype(jnp.float32), pre[:, inner:].astype(jnp.float32)
        act = (gate * jax.nn.sigmoid(gate) * up * spread_weights(chunk)).astype(jnp.bfloat16)
        mixed = jnp.dot(act, w_out, preferred_element_type=jnp.float32).astype(jnp.bfloat16)
        output = (widened + scatter(mixed).astype(jnp.float32)).astype(jnp.bfloat16)
        if tick < ticks - 1:
            incoming = from_behind(output, "section", 1)
        keep(hiddens, hidden, lambda c: tick - c)
        keep(rows_in, gathered, lambda c: tick - c)
        keep(pre_acts, pre, lambda c: tick - c)
        keep(acts, act, lambda c: tick - c)
        keep(outputs, output, lambda c: tick - c)

    grads_in, pre_grads, results = [], [], []
    for tick in range(ticks):
        chunk = jnp.clip(tick - (sections - 1 - section_id), 0, chunks - 1)
        active = {
            s: tick - (sections - 1 - s)
            for s in range(sections)
            if 0 <= tick - (sections - 1 - s) < chunks
        }
        grad_out = None
        if tick < chunks:
            grad_out = chunk_of(cotangent, chunk, 0).reshape(own_rows, width)
        if tick > 0:
            grad_out = incoming if grad_out is None else jnp.where(section_id == sections - 1, grad_out, incoming)
        gathered = gather(grad_out)
        pre = pick(section_id, {s: at(pre_acts, c, s) for s, c in active.items()})
        gate, up = pre[:, :inner].astype(jnp.float32), pre[:, inner:].astype(jnp.float32)
        act_grad = lax.dot_general(
            gathered, w_out, (((1,), (1,)), ((), ())), preferred_element_type=jnp.float32
        )
        act_grad = act_grad * spread_weights(chunk)
        sig = jax.nn.sigmoid(gate)
        pre_grad = jnp.concatenate(
            [
                (act_grad * up * sig * (1.0 + gate * (1.0 - sig))).astype(jnp.bfloat16),
                (act_grad * gate * sig).astype(jnp.bfloat16),
            ],
            axis=1,
        )
        row_grad = lax.dot_general(
            pre_grad, w_in, (((1,), (1,)), ((), ())), preferred_element_type=jnp.float32
        ).astype(jnp.bfloat16)
        dnormed = scatter(row_grad).astype(jnp.float32)
        hidden = pick(section_id, {s: at(hiddens, c, s) for s, c in active.items()})
        widened, inv_rms = rms(hidden)
        unit = widened * inv_rms
        scaled = dnormed * gain_row
        result = (
            grad_out.astype(jnp.float32)
            + inv_rms * (scaled - unit * jnp.mean(scaled * unit, axis=-1, keepdims=True))
        ).astype(jnp.bfloat16)
        if tick < ticks - 1:
            incoming = from_behind(result, "section", -1)
        keep(grads_in, gathered, lambda c: sections - 1 - tick + c)
        keep(pre_grads, pre_grad, lambda c: sections - 1 - tick + c)
        keep(results, result, lambda c: sections - 1 - tick + c)

    def contract(left, right):
        return lax.dot_general(left, right, (((0,), (0,)), ((), ())), preferred_element_type=jnp.float32)

    def summed(pairs):
        total = contract(*pairs[0])
        for pair in pairs[1:]:
            total = total + contract(*pair)
        return total.astype(jnp.bfloat16)


    def split_columns(array, groups, part):
        size = array.shape[1] // groups
        piece = size // dp_count
        cuts = [lax.dynamic_slice_in_dim(array, g * size + part * piece, piece, 1) for g in range(groups)]
        return cuts[0] if groups == 1 else jnp.concatenate(cuts, axis=1)

    def in_weight_part(part):
        def branch(section):
            back = sections - 1 - section
            return lambda: summed(
                [(split_columns(at(rows_in, c, section), 1, part), at(pre_grads, c, back)) for c in range(chunks)]
            )

        if compact:
            return branch(0)()
        return lax.switch(section_id, [branch(s) for s in range(sections)])

    def out_weight_part(part):
        def branch(section):
            back = sections - 1 - section
            return lambda: summed(
                [(split_columns(at(acts, c, section), held, part), at(grads_in, c, back)) for c in range(chunks)]
            )

        if compact:
            return branch(0)()
        return lax.switch(section_id, [branch(s) for s in range(sections)])

    dp_id = lax.axis_index("dp")

    def over_dp(part_fn):
        total = part_fn(dp_id).astype(jnp.float32)
        for distance in range(1, dp_count):
            ring = [(i, (i + distance) % dp_count) for i in range(dp_count)]
            other = part_fn((dp_id + distance) % dp_count)
            total = total + lax.ppermute(other, "dp", ring).astype(jnp.float32)
        return total.astype(jnp.bfloat16)

    out_grads = over_dp(out_weight_part)
    in_grads = over_dp(in_weight_part)
    grad_gate = jnp.stack([in_grads[:, e * hidden_units : (e + 1) * hidden_units] for e in range(held)])
    grad_up = jnp.stack([in_grads[:, inner + e * hidden_units : inner + (e + 1) * hidden_units] for e in range(held)])
    grad_down = out_grads.reshape(held, hidden_units // dp_count, width)

    def in_order(per_tick, first_tick):
        kept = pick(
            section_id,
            {
                s: jnp.concatenate([at(per_tick, c, first_tick(s)) for c in range(chunks)], axis=0)
                for s in range(sections)
            },
        )
        return kept.reshape(1, micro_count, token_rows, width)

    layer_out = in_order(outputs, lambda s: s)
    input_grad = in_order(results, lambda s: sections - 1 - s)
    return (layer_out, input_grad, grad_gate[None], grad_up[None], grad_down[None])


def solution(mesh):
    placed = (
        P(None, ("expert", "dp"), None),
        P(None, ("expert", "dp"), None),
        P("section", None, ("expert", "dp"), None),
        P("section", None, ("expert", "dp"), None),
        P("section", None),
        P("section", "expert", None, None),
        P("section", "expert", None, None),
        P("section", "expert", None, None),
    )
    return jax.shard_map(
        on_device,
        mesh=mesh,
        in_specs=placed,
        out_specs=(
            P("section", None, ("expert", "dp"), None),
            P("section", None, ("expert", "dp"), None),
            P("section", "expert", "dp", None),
            P("section", "expert", "dp", None),
            P("section", "expert", "dp", None),
        ),
        check_vma=False,
    )
```

time: 1400 us -> 768 us (0.55)
  local copies, waits for them, and re-layouts: 208 us -> 22.3 us
  waiting for transfers between devices: 712 us -> 546 us
  starting transfers between devices: 179 us -> 13.5 us
  matrix products: 195 us -> 125 us
  other arithmetic: 83.9 us -> 36.8 us
    all_to_all x36 -> x1, waiting for transfers between devices: 652 us -> 0.07 us  [weight_table(): lax.all_to_all(dense, 'expert', split_axis=0, concat_axis=0, tiled=True)]
    reduce_scatter x3 -> x4, waiting for transfers between devices: 22.5 us -> 272 us  [scatter(): return lax.psum_scatter(rows, 'expert', scatter_dimension=0, tiled=True)]
    all_gather x0 -> x4, waiting for transfers between devices: none -> 249 us  [gather(): return lax.all_gather(rows, 'expert', axis=0, tiled=True)]
    all_to_all x36 -> x1, starting transfers between devices: 133 us -> 7.28 us  [weight_table(): lax.all_to_all(dense, 'expert', split_axis=0, concat_axis=0, tiled=True)]
    dynamic_slice x90 -> x2, local copies, waits for them, and re-layouts: 70.6 us -> 0.28 us  [split_columns(): lax.dynamic_slice_in_dim(array, g * size + part * piece, piece, 1)]
    dot_general x87 -> x12, matrix products: 195 us -> 125 us  [the longest x4 32.7 us: contract(): lax.dot_general(left, right, (((0,), (0,)), ((), ())), preferred_element_...]
    dynamic_update_slice x36 -> x0, other arithmetic: 55.1 us -> none  [keep_slice(): lax.dynamic_update_index_in_dim(stored, jnp.where(is_valid, new_value, pr...]
    ppermute x18 -> x2, starting transfers between devices: 46.1 us -> 4.68 us  [from_behind(): return lax.ppermute(block, axis, route)]
  transfers between devices with their start and end apart: 57 -> 13, of which waited for: 48 -> 11; matrix products, arithmetic and copies ran while one was open for 12% -> 15% of each run, Pallas kernels for 0% -> 0%
where the time goes in v1:
time: 768 us; the launch traced here: 759 us
  waiting for transfers between devices  546 us (71%)
  matrix products  125 us (16%)
  other arithmetic  36.8 us (5%)
  local copies, waits for them, and re-layouts  22.3 us (3%)
  between operations  14.9 us (2%)
  starting transfers between devices  13.5 us (2%)
    reduce_scatter x4, waiting for transfers between devices, scatter(): return lax.psum_scatter(rows, 'expert', scatter_dimension=0, tiled=True)  272 us
    all_gather x4, waiting for transfers between devices, gather(): return lax.all_gather(rows, 'expert', axis=0, tiled=True)  249 us
    dot_general x4, matrix products, contract(): lax.dot_general(left, right, (((0,), (0,)), ((), ())), preferred_element_...  32.7 us
    dot_general x2, matrix products, on_device(): jnp.dot(gathered, w_in, preferred_element_type=jnp.float32)  27.3 us
    dot_general x2, matrix products, on_device(): lax.dot_general(pre_grad, w_in, (((1,), (1,)), ((), ())), preferred_eleme...  25.3 us
    ppermute x2, waiting for transfers between devices, from_behind(): return lax.ppermute(block, axis, route)  24.6 us
    dot_general x2, matrix products, on_device(): lax.dot_general(gathered, w_out, (((1,), (1,)), ((), ())), preferred_elem...  24.2 us
    dot_general x2, matrix products, on_device(): jnp.dot(act, w_out, preferred_element_type=jnp.float32).astype(jnp.bfloat16)  15.5 us
  transfers between devices with their start and end apart: 13, of which 11 were waited for; matrix products, arithmetic and copies ran while one was open for 15% of the time, Pallas kernels for 0%

profile of v1, /device:TPU:0, one launch (start us, length us, event | category | flops | bytes accessed | tf_op | source)
XLA Modules:
  0.0 759.2 jit_solution(15389432934267854801)
XLA Ops:
  8.5 2.0 fusion.66
  12.2 7.3 all-to-all-start
  19.6 6.5 slice_bitcast_fusion.1
  28.0 1.4 broadcast_in_dim.36
  29.4 3.0 copy.35
  32.4 53.9 %all-gather.5.cloned.1.call-done = bf16[1024,2048]{1,0:T(8,128)(2,1)} async-done(((bf16[128,2048]{1,0:T(8,128)(2,1)}), bf16[1024,2048]{1,0:T(8,128)(2,1)}) %all-gather.5.cloned.1.call-update) | async-done | bytes 4194320 | tf_op jit(solution)/shard_map/all_gather | solution.py:61
  86.3 13.0 %convolution_convert_fusion.5 = bf16[1024,2048]{1,0:T(8,128)(2,1)S(1)} fusion(bf16[1024,2048]{1,0:T(8,128)(2,1)} %all-gather.5.cloned.1.call-done, bf16[2048,512]{1,0:T(8,128)(2,1)} %get-tuple-element.115, bf16[2048,512]{1,0:T(8,128)(2,1)S(1)} %get-tuple-element.114, bf16[2048,512]{1,0:T(8,128)(2,1)} %get-tuple-element.116, ...), kind=kOutput, calls=%fused_computation.84 | convolution fusion | flops 8625586176 | bytes 16777216 | tf_op jit(solution)/shard_map/dot_general | solution.py:95
  99.3 1.5 fusion.31
  101.4 1.6 copy-done.22
  103.0 6.2 convolution_convert_fusion.7
  109.3 87.0 %reduce-scatter.5.cloned.1.call-done = bf16[128,2048]{1,0:T(8,128)(2,1)} async-done(((bf16[1024,2048]{1,0:T(8,128)(2,1)}), bf16[128,2048]{1,0:T(8,128)(2,1)}) %reduce-scatter.5.cloned.1.call-update) | async-done | bytes 524304 | tf_op jit(solution)/shard_map/reduce_scatter | solution.py:64
  197.4 3.4 collective-permute-start
  200.8 10.8 %collective-permute-done = bf16[128,2048]{1,0:T(8,128)(2,1)S(1)} collective-permute-done((bf16[128,2048]{1,0:T(8,128)(2,1)S(1)}, bf16[128,2048]{1,0:T(8,128)(2,1)S(1)}, u32[]{:S(2)}, u32[]{:S(2)}) %collective-permute-start) | collective-permute-done | bytes 524320 | tf_op jit(solution)/shard_map/ppermute | solution.py:13
  213.6 73.3 %all-gather.7.cloned.1.call-done = bf16[1024,2048]{1,0:T(8,128)(2,1)} async-done(((bf16[128,2048]{1,0:T(8,128)(2,1)}), bf16[1024,2048]{1,0:T(8,128)(2,1)}) %all-gather.7.cloned.1.call-update) | async-done | bytes 4194320 | tf_op jit(solution)/shard_map/all_gather | solution.py:61
  286.9 14.3 %convolution_convert_fusion.4 = bf16[1024,2048]{1,0:T(8,128)(2,1)} fusion(bf16[1024,2048]{1,0:T(8,128)(2,1)} %all-gather.7.cloned.1.call-done, bf16[2048,512]{1,0:T(8,128)(2,1)} %get-tuple-element.115, bf16[2048,512]{1,0:T(8,128)(2,1)} %copy-done.18, bf16[2048,512]{1,0:T(8,128)(2,1)} %get-tuple-element.116, bf16[2048,512]{1,0:T(8,128)(2,1)} %get-tuple-element.117), kind=kOutput, calls=%fused_computation.83 | convolution fusion | flops 8625586176 | bytes 16777216 | tf_op jit(solution)/shard_map/dot_general | solution.py:95
  301.2 59.1 %all-gather.9.cloned.1.call-done = bf16[1024,2048]{1,0:T(8,128)(2,1)} async-done(((bf16[128,2048]{1,0:T(8,128)(2,1)}), bf16[1024,2048]{1,0:T(8,128)(2,1)}) %all-gather.9.cloned.1.call-update) | async-done | bytes 4194320 | tf_op jit(solution)/shard_map/all_gather | solution.py:61
  360.3 12.3 %fusion.39 = (bf16[1024,1024]{1,0:T(8,128)(2,1)S(1)}, bf16[1024,1024]{1,0:T(8,128)(2,1)S(1)}, bf16[1024,1024]{1,0:T(8,128)(2,1)}) fusion(bf16[1024,2048]{1,0:T(8,128)(2,1)} %convolution_convert_fusion.4, f32[1024,1024]{1,0:T(8,128)} %bitcast.77, bf16[1024,2048]{1,0:T(8,128)(2,1)} %all-gather.9.cloned.1.call-done, bf16[1024,2048]{1,0:T(8,128)(2,1)} %bitcast.96), kind=kOutput, calls=%fused_computation.65 | convolution fusion | flops 4315938816 | bytes 23068672 | tf_op jit(solution)/shard_map/dot_general | solution.py:124
  372.6 1.3 copy-done.10
  374.6 12.6 %convolution_convert_fusion.3 = bf16[1024,2048]{1,0:T(8,128)(2,1)} fusion(bf16[1024,1024]{1,0:T(8,128)(2,1)S(1)} %get-tuple-element.106, bf16[1024,1024]{1,0:T(8,128)(2,1)S(1)} %get-tuple-element.105, bf16[2048,512]{1,0:T(8,128)(2,1)} %get-tuple-element.115, bf16[2048,512]{1,0:T(8,128)(2,1)} %copy-done.18, bf16[2048,512]{1,0:T(8,128)(2,1)} %get-tuple-element.116, ...), kind=kOutput, calls=%fused_computation.82 | convolution fusion | flops 8633974784 | bytes 16777216 | tf_op jit(solution)/shard_map/dot_general | solution.py:136
  387.3 86.9 %reduce-scatter.9.cloned.1.call-done = bf16[128,2048]{1,0:T(8,128)(2,1)} async-done(((bf16[1024,2048]{1,0:T(8,128)(2,1)}), bf16[128,2048]{1,0:T(8,128)(2,1)}) %reduce-scatter.9.cloned.1.call-update) | async-done | bytes 524304 | tf_op jit(solution)/shard_map/reduce_scatter | solution.py:64
  474.2 1.4 fusion.56
  475.6 1.5 fusion.60
  477.9 1.3 collective-permute-start.1
  479.2 13.9 %collective-permute-done.1 = bf16[128,2048]{1,0:T(8,128)(2,1)S(1)} collective-permute-done((bf16[128,2048]{1,0:T(8,128)(2,1)S(1)}, bf16[128,2048]{1,0:T(8,128)(2,1)S(1)}, u32[]{:S(2)}, u32[]{:S(2)}) %collective-permute-start.1) | collective-permute-done | bytes 524320 | tf_op jit(solution)/shard_map/ppermute | solution.py:13
  494.4 9.4 %convolution_convert_fusion.6 = bf16[1024,2048]{1,0:T(8,128)(2,1)} fusion(bf16[1024,1024]{1,0:T(8,128)(2,1)} %get-tuple-element.111, bf16[1024,2048]{1,0:T(8,128)(2,1)} %bitcast.97), kind=kOutput, calls=%fused_computation.85 | convolution fusion | flops 4297064448 | bytes 10485760 | tf_op jit(solution)/shard_map/dot_general | solution.py:98
  503.8 62.4 %all-gather.11.cloned.1.call-done = bf16[1024,2048]{1,0:T(8,128)(2,1)} async-done(((bf16[128,2048]{1,0:T(8,128)(2,1)}), bf16[1024,2048]{1,0:T(8,128)(2,1)}) %all-gather.11.cloned.1.call-update) | async-done | bytes 4194320 | tf_op jit(solution)/shard_map/all_gather | solution.py:61
  566.1 11.9 %fusion.34 = (bf16[1024,1024]{1,0:T(8,128)(2,1)S(1)}, bf16[1024,1024]{1,0:T(8,128)(2,1)S(1)}) fusion(bf16[1024,2048]{1,0:T(8,128)(2,1)} %copy-done.4, f32[1024,1024]{1,0:T(8,128)} %bitcast.78, bf16[1024,2048]{1,0:T(8,128)(2,1)} %all-gather.11.cloned.1.call-done, bf16[1024,2048]{1,0:T(8,128)(2,1)} %bitcast.98), kind=kOutput, calls=%fused_computation.60 | convolution fusion | flops 4311744512 | bytes 20971520 | tf_op jit(solution)/shard_map/dot_general | solution.py:124
  578.0 1.3 copy-done.12
  580.0 12.7 %convolution_convert_fusion.2 = bf16[1024,2048]{1,0:T(8,128)(2,1)} fusion(bf16[1024,1024]{1,0:T(8,128)(2,1)S(1)} %get-tuple-element.104, bf16[1024,1024]{1,0:T(8,128)(2,1)S(1)} %get-tuple-element.103, bf16[2048,512]{1,0:T(8,128)(2,1)} %get-tuple-element.115, bf16[2048,512]{1,0:T(8,128)(2,1)} %copy-done.18, bf16[2048,512]{1,0:T(8,128)(2,1)} %get-tuple-element.116, ...), kind=kOutput, calls=%fused_computation.81 | convolution fusion | flops 8633974784 | bytes 16777216 | tf_op jit(solution)/shard_map/dot_general | solution.py:136
  592.8 5.1 pad_maximum_fusion.1
  597.9 2.4 pad_maximum_fusion.2
  600.3 9.6 %conditional.13 = (bf16[1024,2048]{1,0:T(8,128)(2,1)}) conditional(s32[]{:T(128)} %clamp.2, (s32[]{:T(128)}, bf16[1024,2048]{1,0:T(8,128)(2,1)}, bf16[1024,2048]{1,0:T(8,128)(2,1)}) %tuple.44, (s32[]{:T(128)}, bf16[1024,2048]{1,0:T(8,128)(2,1)}, bf16[1024,2048]{1,0:T(8,128)(2,1)}) %tuple.45), branch_computations={%region_11.12_spmd, %region_12.13_spmd} | conditional | flops 4294967296 | bytes 10485818
  600.5 9.4 %fusion.4 = bf16[1024,2048]{1,0:T(8,128)(2,1)} fusion(bf16[1024,2048]{1,0:T(8,128)(2,1)} %get-tuple-element.74, bf16[1024,2048]{1,0:T(8,128)(2,1)} %get-tuple-element.72, s32[]{:T(128)S(6)} %select_n.46), kind=kOutput, calls=%fused_computation.6 | convolution fusion | flops 4294967296 | bytes 10485764 | tf_op jit(solution)/shard_map/cond/branch_0_fun/dot_general | solution.py:155
  609.9 6.3 conditional.15
  610.0 6.0 fusion.20
  616.8 39.9 %reduce-scatter.7.cloned.1.call-done = bf16[128,2048]{1,0:T(8,128)(2,1)} async-done(((bf16[1024,2048]{1,0:T(8,128)(2,1)}), bf16[128,2048]{1,0:T(8,128)(2,1)}) %reduce-scatter.7.cloned.1.call-update) | async-done | bytes 524304 | tf_op jit(solution)/shard_map/reduce_scatter | solution.py:64
  656.7 2.1 fusion.75
  658.7 10.7 %conditional.12 = (f32[1024,2048]{1,0:T(8,128)}) conditional(s32[]{:T(128)} %clamp.2, (s32[]{:T(128)}, bf16[1024,2048]{1,0:T(8,128)(2,1)}, bf16[1024,2048]{1,0:T(8,128)(2,1)}) %tuple.42, (s32[]{:T(128)}, bf16[1024,2048]{1,0:T(8,128)(2,1)}, bf16[1024,2048]{1,0:T(8,128)(2,1)}) %tuple.43), branch_computations={%region_9.10_spmd, %region_10.11_spmd} | conditional | flops 4299161600 | bytes 14680122 | solution.py:179
  658.7 10.7 %convert_convert_fusion = f32[1024,2048]{1,0:T(8,128)} fusion(bf16[1024,2048]{1,0:T(8,128)(2,1)} %get-tuple-element.68, bf16[1024,2048]{1,0:T(8,128)(2,1)} %get-tuple-element.66, s32[]{:T(128)S(6)} %select_n.44), kind=kOutput, calls=%fused_computation | convolution fusion | flops 4299161600 | bytes 14680068 | tf_op jit(solution)/shard_map/cond/branch_0_fun/dot_general | solution.py:155
  669.4 7.0 conditional.14
  669.8 6.6 fusion.10
  676.4 5.1 add_convert_fusion.1
  682.6 3.8 add_convert_fusion
  686.8 1.5 maximum_bitcast_fusion
  688.3 1.5 maximum_bitcast_fusion.1
  689.8 58.4 %reduce-scatter.11.cloned.1.call-done = bf16[128,2048]{1,0:T(8,128)(2,1)} async-done(((bf16[1024,2048]{1,0:T(8,128)(2,1)}), bf16[128,2048]{1,0:T(8,128)(2,1)}) %reduce-scatter.11.cloned.1.call-update) | async-done | bytes 524304 | tf_op jit(solution)/shard_map/reduce_scatter | solution.py:64
  748.2 1.4 fusion.67
  749.6 2.3 fusion.74
  (82 shorter events, 14.7 us)
Async XLA Ops:
  7.2 79.1 %all-gather.5.cloned.1.call-start = ((), (), s32[]{:S(2)}) async-start(), calls=%async_computation.5 | async-start | bytes 4718592 | tf_op jit(solution)/shard_map/all_gather | solution.py:61
  8.5 2.1 copy-start.20
  12.2 13.9 %all-to-all-start = ((f32[8,1,256]{2,1,0:T(1,128)}), f32[8,1,256]{2,1,0:T(1,128)S(1)}, u32[]{:S(2)}, u32[]{:S(2)}) async-start(f32[8,1,256]{2,1,0:T(1,128)} %reshape.77), calls=%async_computation | async-start | bytes 16384 | tf_op jit(solution)/shard_map/all_to_all | solution.py:29
  19.5 176.7 %reduce-scatter.5.cloned.1.call-start = ((), (), s32[]{:S(2)}) async-start(), calls=%async_computation.6 | async-start | bytes 4718592 | tf_op jit(solution)/shard_map/reduce_scatter | solution.py:64
  26.1 60.2 %copy-start.18 = (bf16[2048,512]{1,0:T(8,128)(2,1)}, bf16[2048,512]{1,0:T(8,128)(2,1)S(1)}, u32[]{:S(2)}) copy-start(bf16[2048,512]{1,0:T(8,128)(2,1)S(1)} %get-tuple-element.114) | copy-start | bytes 6291460
  86.3 13.1 %copy-start = (f32[128,8,2,512]{3,1,2,0:T(8,128)S(1)}, f32[128,8,2,512]{3,1,2,0:T(8,128)}, u32[]{:S(2)}) copy-start(f32[128,8,2,512]{3,1,2,0:T(8,128)} %copy.35) | copy-start | bytes 12582916
  99.3 2.1 copy-start.4
  99.3 3.7 copy-start.22
  109.2 87.0 %copy-start.1 = (bf16[8,16,2048]{2,1,0:T(8,128)(2,1)S(1)}, bf16[8,16,2048]{2,1,0:T(8,128)(2,1)}, u32[]{:S(2)}) copy-start(bf16[8,16,2048]{2,1,0:T(8,128)(2,1)} %param.16) | copy-start | bytes 1572868
  109.2 102.6 %copy-start.19 = (f32[1,2048]{1,0:T(1,128)S(1)}, f32[1,2048]{1,0:T(1,128)}, u32[]{:S(2)}) copy-start(f32[1,2048]{1,0:T(1,128)} %param.20) | copy-start | bytes 24580
  109.2 177.7 %all-gather.7.cloned.1.call-start = ((), (), s32[]{:S(2)}) async-start(), calls=%async_computation.7 | async-start | bytes 4718592 | tf_op jit(solution)/shard_map/all_gather | solution.py:61
  197.4 14.2 %copy-start.5 = (bf16[128,2048]{1,0:T(8,128)(2,1)}, bf16[128,2048]{1,0:T(8,128)(2,1)S(1)}, u32[]{:S(2)}) copy-start(bf16[128,2048]{1,0:T(8,128)(2,1)S(1)} %fusion.73) | copy-start | bytes 1572868
  197.4 14.2 %collective-permute-start = (bf16[128,2048]{1,0:T(8,128)(2,1)S(1)}, bf16[128,2048]{1,0:T(8,128)(2,1)S(1)}, u32[]{:S(2)}, u32[]{:S(2)}) collective-permute-start(bf16[128,2048]{1,0:T(8,128)(2,1)S(1)} %fusion.73), channel_id=1, source_target_pairs={{0,16},{1,17},{2,18},{3,19},{4,20},{5,21},{6,22},{7,23},{8,24},{9,... | collective-permute-start | bytes 1572872 | tf_op jit(solution)/shard_map/ppermute | solution.py:13
  212.8 147.5 %all-gather.9.cloned.1.call-start = ((), (), s32[]{:S(2)}) async-start(), calls=%async_computation.9 | async-start | bytes 4718592 | tf_op jit(solution)/shard_map/all_gather | solution.py:61
  213.4 260.8 %reduce-scatter.9.cloned.1.call-start = ((), (), s32[]{:S(2)}) async-start(), calls=%async_computation.10 | async-start | bytes 4718592 | tf_op jit(solution)/shard_map/reduce_scatter | solution.py:64
  372.6 1.3 copy-start.10
  372.6 2.0 copy-start.11
  387.2 88.4 %copy-start.7 = (bf16[8,16,2048]{2,1,0:T(8,128)(2,1)S(1)}, bf16[8,16,2048]{2,1,0:T(8,128)(2,1)}, u32[]{:S(2)}) copy-start(bf16[8,16,2048]{2,1,0:T(8,128)(2,1)} %param.17) | copy-start | bytes 1572868
  387.2 178.9 %all-gather.11.cloned.1.call-start = ((), (), s32[]{:S(2)}) async-start(), calls=%async_computation.11 | async-start | bytes 4718592 | tf_op jit(solution)/shard_map/all_gather | solution.py:61
  477.0 0.8 copy-start.16
  477.9 15.2 %collective-permute-start.1 = (bf16[128,2048]{1,0:T(8,128)(2,1)S(1)}, bf16[128,2048]{1,0:T(8,128)(2,1)S(1)}, u32[]{:S(2)}, u32[]{:S(2)}) collective-permute-start(bf16[128,2048]{1,0:T(8,128)(2,1)S(1)} %fusion.60), channel_id=1, source_target_pairs={{16,0},{17,1},{18,2},{19,3},{20,4},{21,5},{22,6},{23,7},{24,8},{25... | collective-permute-start | bytes 1572872 | tf_op jit(solution)/shard_map/ppermute | solution.py:13
  493.0 0.8 copy-start.8
  493.9 162.8 %reduce-scatter.7.cloned.1.call-start = ((), (), s32[]{:S(2)}) async-start(), calls=%async_computation.8 | async-start | bytes 4718592 | tf_op jit(solution)/shard_map/reduce_scatter | solution.py:64
  503.7 244.5 %reduce-scatter.11.cloned.1.call-start = ((), (), s32[]{:S(2)}) async-start(), calls=%async_computation.12 | async-start | bytes 4718592 | tf_op jit(solution)/shard_map/reduce_scatter | solution.py:64
  578.0 1.3 copy-start.12
  578.0 2.0 copy-start.14
  592.7 5.1 copy-start.13
  592.8 5.1 copy-start.15
  609.9 71.7 %collective-permute-start.2 = (bf16[1024,2048]{1,0:T(8,128)(2,1)}, bf16[1024,2048]{1,0:T(8,128)(2,1)}, u32[]{:S(2)}, u32[]{:S(2)}) collective-permute-start(bf16[1024,2048]{1,0:T(8,128)(2,1)} %get-tuple-element.119), channel_id=1, source_target_pairs={{0,1},{1,0},{2,3},{3,2},{4,5},{5,4},{6,7},{7,6},{8,9},{9,8},{10,11... | collective-permute-start | bytes 12582920 | tf_op jit(solution)/shard_map/ppermute | solution.py:199
  609.9 46.8 %copy-start.6 = (bf16[128,2048]{1,0:T(8,128)(2,1)S(1)}, bf16[128,2048]{1,0:T(8,128)(2,1)}, u32[]{:S(2)}) copy-start(bf16[128,2048]{1,0:T(8,128)(2,1)} %copy-done.5) | copy-start | bytes 1572868
  616.2 60.2 %collective-permute-start.3 = (bf16[512,2048]{1,0:T(8,128)(2,1)}, bf16[512,2048]{1,0:T(8,128)(2,1)}, u32[]{:S(2)}, u32[]{:S(2)}) collective-permute-start(bf16[512,2048]{1,0:T(8,128)(2,1)} %get-tuple-element.121), channel_id=1, source_target_pairs={{0,1},{1,0},{2,3},{3,2},{4,5},{5,4},{6,7},{7,6},{8,9},{9,8},{10,11... | collective-permute-start | bytes 6291464 | tf_op jit(solution)/shard_map/ppermute | solution.py:199
  676.4 6.2 copy-start.3
  686.8 61.5 %copy-start.2 = (bf16[8,16,2048]{2,1,0:T(8,128)(2,1)S(1)}, bf16[8,16,2048]{2,1,0:T(8,128)(2,1)}, u32[]{:S(2)}) copy-start(bf16[8,16,2048]{2,1,0:T(8,128)(2,1)} %param.16) | copy-start | bytes 1572868
  686.8 61.5 %copy-start.21 = (f32[128]{0:T(128)S(1)}, f32[128]{0:T(128)}, u32[]{:S(2)}) copy-start(f32[128]{0:T(128)} %copy-done.20) | copy-start | bytes 1540
  686.8 62.8 %copy-start.9 = (bf16[128,2048]{1,0:T(8,128)(2,1)S(1)}, bf16[128,2048]{1,0:T(8,128)(2,1)}, u32[]{:S(2)}) copy-start(bf16[128,2048]{1,0:T(8,128)(2,1)} %copy-done.8) | copy-start | bytes 1572868
  686.8 62.8 %copy-start.17 = (bf16[128,2048]{1,0:T(8,128)(2,1)S(1)}, bf16[128,2048]{1,0:T(8,128)(2,1)}, u32[]{:S(2)}) copy-start(bf16[128,2048]{1,0:T(8,128)(2,1)} %copy-done.16) | copy-start | bytes 1572868
Sparse Core Ops, SparseCore 0:
  10.7 75.4 all-gather.4
  109.3 86.8 reduce-scatter.4
  212.9 73.9 all-gather.6
  288.9 71.3 all-gather.8
  387.3 86.8 reduce-scatter.8
  494.0 72.0 all-gather.10
  569.8 86.8 reduce-scatter.6
  660.3 87.9 reduce-scatter.10
